TPU v7x, 32 devices: a whole 2x2x4 slice. The times are simulated.
32 devices in a mesh: ep: 8 (over y, x, core), tp: 4 (over z).
Axes of the slice: x: 2, y: 2, z: 4, core: 2. Of those that a mesh axis runs over, the one named last changes fastest.
Arguments:
- latents: bfloat16 [64, 1024], P('ep'), may hold values from -6 to 6
- expert_ids: int32 [64, 22], P('ep'), may hold values from 0 to 127, all different within a row; in each aligned block of 8 rows (0 to 7, 8 to 15, ...) at most 3 rows name the same one
- gate_values: float32 [64, 22], P('ep'), may hold values from 0.05 to 0.5
- w_up: bfloat16 [128, 1024, 2688], P('ep', None, 'tp'), may hold values from -0.1875 to 0.1875
- w_down: bfloat16 [128, 2688, 1024], P('ep', 'tp'), may hold values from -0.125 to 0.125
Outputs:
- mixed_rows: bfloat16 [64, 1024], P('ep', 'tp')
Inputs may be any that keep to these rules, and one draw needn't show every extreme that they name: `expert_ids`: each row names 22 different experts. Among the 8 tokens of one index of ep no expert is named more than 3 times, a bound that some block reaches.
All inputs are finite; a program needn't handle non-finite values.
Results may differ from a plain program's by a relative error of at most 0.014.
Values may be sent and summed in bfloat16 or wider, within the bound.
No kernel may reach another device: no remote copies, remote signals or barrier semaphores. Data moves between devices by JAX's collectives and lax.ppermute only.
A program may use at most 128 MiB of HBM per device.

v0:
```python
import jax
import jax.numpy as jnp
from jax import lax
from jax.sharding import PartitionSpec as P


def expert_block(inputs, w_up, w_down):
    preact = jnp.einsum("abck,bkf->abcf", inputs, w_up, preferred_element_type=jnp.float32)
    hidden = jnp.square(jnp.maximum(preact, 0.0)).astype(jnp.bfloat16)
    return jnp.einsum("abcf,bfk->abck", hidden, w_down, preferred_element_type=jnp.float32)


def per_device(latents, expert_ids, gate_values, w_up, w_down):
    ep_count = lax.axis_size("ep")
    tp_count = lax.axis_size("tp")
    token_count = expert_ids.shape[0]
    exp_local = w_up.shape[0]
    model_width = w_up.shape[1]
    expert_total = exp_local * ep_count
    slot_most = 3 * token_count // 8
    slot_total = expert_total * slot_most
    quarter = model_width // tp_count
    labels = jnp.arange(expert_total, dtype=jnp.int32)
    chosen = (expert_ids[:, :, None] == labels[None, None, :]).astype(jnp.int32)
    named_count = jnp.sum(chosen, axis=1)
    before = jnp.cumsum(named_count, axis=0) - named_count
    slot_index = jnp.sum(chosen * before[:, None, :], axis=2)
    row_index = expert_ids * slot_most + slot_index
    row_hit = row_index[:, :, None] == jnp.arange(slot_total, dtype=jnp.int32)[None, None, :]
    select = jnp.sum(row_hit.astype(jnp.int32), axis=1).astype(jnp.bfloat16)
    outgoing = jnp.einsum("ts,tk->sk", select, latents, preferred_element_type=jnp.float32).astype(
        jnp.bfloat16
    )
    outgoing = outgoing.reshape(ep_count, exp_local, slot_most, model_width)
    partial_out = expert_block(
        lax.all_to_all(outgoing, "ep", split_axis=0, concat_axis=0, tiled=True), w_up, w_down
    )
    gate_hit = row_hit.astype(jnp.float32)
    summed = lax.psum_scatter(
        partial_out.astype(jnp.bfloat16), "tp", scatter_dimension=3, tiled=True
    )
    back_rows = lax.all_to_all(summed, "ep", split_axis=0, concat_axis=0, tiled=True)
    back_rows = back_rows.reshape(slot_total, quarter).astype(jnp.float32)
    weights = jnp.sum(gate_values[:, :, None] * gate_hit, axis=1)
    mixed_rows = jnp.dot(weights, back_rows, precision=lax.Precision.HIGHEST)
    return mixed_rows.astype(jnp.bfloat16)


def solution(mesh):
    return jax.shard_map(
        per_device,
        mesh=mesh,
        in_specs=(
            P("ep", None),
            P("ep", None),
            P("ep", None),
            P("ep", None, "tp"),
            P("ep", "tp", None),
        ),
        out_specs=P("ep", "tp"),
        check_vma=False,
    )
```

profile of v0, /device:TPU:0, one launch (start us, length us, event | category | flops | bytes accessed | tf_op | source)
XLA Modules:
  0.0 87.2 jit_solution(5816546831841071648)
XLA Ops:
  6.5 0.0 copy-start
  6.5 0.0 reduce-scatter.2.cloned.1.call-start
  6.5 0.8 copy.14
  7.3 0.1 convert_reduce_fusion.1
  7.5 0.5 select_reduce_fusion.1
  8.0 0.1 convert_reduce_fusion
  8.1 0.0 copy-done
  8.1 0.4 convolution_convert_fusion
  8.5 0.5 reshape.18
  9.0 0.3 copy.17
  9.3 17.5 %all_to_all.10 = bf16[8,16,3,1024]{3,1,2,0:T(8,128)(2,1)S(1)} all-to-all(bf16[8,16,3,1024]{3,1,2,0:T(8,128)(2,1)S(1)} %copy.17), channel_id=1, replica_groups=mesh['ep'=8,'tp'=4] {'ep'}, dimensions={0} | all-to-all | bytes 1572864 | tf_op jit(solution)/shard_map/all_to_all | solution.py:36
  26.9 0.0 copy-start.1
  26.9 18.2 %fusion.7 = bf16[8,16,3,1024]{3,0,2,1:T(8,128)(2,1)} fusion(bf16[16,672,1024]{2,1,0:T(8,128)(2,1)} %param.9, bf16[16,1024,672]{1,2,0:T(8,128)(2,1)} %param.8, bf16[8,16,3,1024]{3,1,2,0:T(8,128)(2,1)S(1)} %all_to_all.10), kind=kOutput, calls=%fused_computation.6 | convolution fusion | flops 1058131968 | bytes 45613056 | tf_op jit(solution)/shard_map/abcf,bfk->abck/dot_general | solution.py:10
  45.1 0.0 reduce-scatter.2.cloned.1.call-update
  45.1 22.7 %reduce-scatter.2.cloned.1.call-done = bf16[8,16,3,256]{3,0,2,1:T(8,128)(2,1)} async-done(((bf16[8,16,3,1024]{3,0,2,1:T(8,128)(2,1)}), bf16[8,16,3,256]{3,0,2,1:T(8,128)(2,1)}) %reduce-scatter.2.cloned.1.call-update) | async-done | bytes 196624 | tf_op jit(solution)/shard_map/reduce_scatter | solution.py:39
  67.8 1.6 %copy.19 = bf16[8,16,3,256]{3,1,2,0:T(8,128)(2,1)} copy(bf16[8,16,3,256]{3,0,2,1:T(8,128)(2,1)} %reduce-scatter.2.cloned.1.call-done) | data formatting | bytes 393216 | tf_op jit(solution)/shard_map/reduce_scatter | solution.py:39
  69.4 3.6 %all-to-all-start.1 = ((bf16[8,16,3,256]{3,1,2,0:T(8,128)(2,1)}), bf16[8,16,3,256]{3,1,2,0:T(8,128)(2,1)S(1)}, u32[]{:S(2)}, u32[]{:S(2)}) async-start(bf16[8,16,3,256]{3,1,2,0:T(8,128)(2,1)} %copy.19), calls=%async_computation.2 | async-start | bytes 393216 | tf_op jit(solution)/shard_map/all_to_all | solution.py:42
  73.1 0.0 copy-done.1
  73.1 0.1 copy.16
  73.2 0.1 select_reduce_fusion
  73.3 6.0 %all-to-all-done.1 = bf16[8,16,3,256]{3,1,2,0:T(8,128)(2,1)S(1)} async-done(((bf16[8,16,3,256]{3,1,2,0:T(8,128)(2,1)}), bf16[8,16,3,256]{3,1,2,0:T(8,128)(2,1)S(1)}, u32[]{:S(2)}, u32[]{:S(2)}) %all-to-all-start.1) | async-done | bytes 196640 | tf_op jit(solution)/shard_map/all_to_all | solution.py:42
  79.3 0.1 copy.20
  79.4 0.2 reshape.19
  79.6 0.8 convolution_convert_fusion.1
  (3 shorter events, 0.0 us)
Async XLA Ops:
  6.5 1.6 %copy-start = (bf16[8,1024]{1,0:T(8,128)(2,1)S(1)}, bf16[8,1024]{1,0:T(8,128)(2,1)}, u32[]{:S(2)}) copy-start(bf16[8,1024]{1,0:T(8,128)(2,1)} %param.5) | copy-start | bytes 49156
  6.5 61.3 %reduce-scatter.2.cloned.1.call-start = ((), (), s32[]{:S(2)}) async-start(), calls=%async_computation.3 | async-start | bytes 983040 | tf_op jit(solution)/shard_map/reduce_scatter | solution.py:39
  26.9 46.2 %copy-start.1 = (f32[8,22]{1,0:T(8,128)S(1)}, f32[8,22]{1,0:T(8,128)}, u32[]{:S(2)}) copy-start(f32[8,22]{1,0:T(8,128)} %param.7) | copy-start | bytes 2116
  69.4 9.8 %all-to-all-start.1 = ((bf16[8,16,3,256]{3,1,2,0:T(8,128)(2,1)}), bf16[8,16,3,256]{3,1,2,0:T(8,128)(2,1)S(1)}, u32[]{:S(2)}, u32[]{:S(2)}) async-start(bf16[8,16,3,256]{3,1,2,0:T(8,128)(2,1)} %copy.19), calls=%async_computation.2 | async-start | bytes 393216 | tf_op jit(solution)/shard_map/all_to_all | solution.py:42
Sparse Core Ops, SparseCore 0:
  45.2 22.5 reduce-scatter.1
where the time goes:
time: 87.5 us; the launch traced here: 87.2 us
  waiting for transfers between devices  28.7 us (33%)
  matrix products  19.4 us (22%)
  blocking collectives  17.5 us (20%)
  between operations  13.5 us (15%)
  local copies, waits for them, and re-layouts  3.63 us (4%)
  starting transfers between devices  3.63 us (4%)
    reduce_scatter x1, waiting for transfers between devices, per_device(): lax.psum_scatter(partial_out.astype(jnp.bfloat16), 'tp', scatter_dimensio...  22.7 us
    dot_general x1, matrix products, expert_block(): jnp.einsum('abcf,bfk->abck', hidden, w_down, preferred_element_type=jnp.f...  18.2 us
    all_to_all x1, blocking collectives, per_device(): lax.all_to_all(outgoing, 'ep', split_axis=0, concat_axis=0, tiled=True)  17.5 us
    all_to_all x1, waiting for transfers between devices, per_device(): lax.all_to_all(summed, 'ep', split_axis=0, concat_axis=0, tiled=True)  5.99 us
    all_to_all x1, starting transfers between devices, per_device(): lax.all_to_all(summed, 'ep', split_axis=0, concat_axis=0, tiled=True)  3.63 us
  transfers between devices with their start and end apart: 2, of which 2 were waited for; matrix products, arithmetic and copies ran while one was open for 0% of the time, Pallas kernels for 0%

commit v1 on v0

v1 whole, which is shorter than its diff:
```python
import functools

import jax
import jax.numpy as jnp
from jax import lax
from jax.experimental import pallas as pl
from jax.experimental.pallas import tpu as pltpu
from jax.sharding import PartitionSpec as P


NT = (((1,), (1,)), ((), ()))
TN = (((0,), (0,)), ((), ()))
VMEM = pl.BlockSpec(memory_space=pltpu.VMEM)
HBM = pl.BlockSpec(memory_space=pltpu.HBM)
DIRECT = 8


def pack_kernel(expert_total, latents_hbm, ids_hbm, gates_hbm, packed, ids, gates, sems):
    tokens, width = latents_hbm.shape
    copies = [
        pltpu.make_async_copy(ids_hbm, ids, sems.at[0]),
        pltpu.make_async_copy(gates_hbm, gates, sems.at[1]),
        pltpu.make_async_copy(latents_hbm, packed.at[:, :width], sems.at[2]),
    ]
    for copy in copies:
        copy.start()
    copies[0].wait()
    copies[1].wait()
    lanes = lax.broadcasted_iota(jnp.int32, (tokens, expert_total), 1)
    dense = jnp.zeros((tokens, expert_total), jnp.float32)
    for k in range(ids.shape[1]):
        dense += jnp.where(ids[:, k : k + 1] == lanes, gates[:, k : k + 1], 0.0)
    lead = dense.astype(jnp.bfloat16)
    packed[:, width : width + expert_total] = lead
    packed[:, width + expert_total :] = (dense - lead.astype(jnp.float32)).astype(jnp.bfloat16)
    copies[2].wait()


def load_kernel(rows_hbm, rows, sems):
    copies = [
        pltpu.make_async_copy(rows_hbm.at[e], rows.at[e], sems.at[e]) for e in range(rows.shape[0])
    ]
    for copy in copies:
        copy.start()
    for copy in copies:
        copy.wait()


def expert_kernel(flips, own, other, up_head, up_hbm, down_hbm, partial, up_tail, down_rows, packed, hidden, total, sems):
    experts, units, width = down_hbm.shape
    head = up_head.shape[0]
    tokens = packed.shape[0]
    expert_total = (packed.shape[1] - width) // 2
    up_copies = [
        pltpu.make_async_copy(up_hbm.at[e], up_tail.at[e - head], sems.at[0, e])
        for e in range(head, experts)
    ]
    down_copies = [
        pltpu.make_async_copy(down_hbm.at[e], down_rows.at[e], sems.at[1, e])
        for e in range(experts)
    ]
    for copy in up_copies + down_copies:
        copy.start()
    packed[: own.shape[0]] = own[...]
    packed[own.shape[0] :] = other[...]
    me = lax.axis_index("ep")
    shape = (max(8, experts), expert_total)
    pick = lax.broadcasted_iota(jnp.int32, shape, 1) == (
        me * experts + lax.broadcasted_iota(jnp.int32, shape, 0)
    )
    pick = pick.astype(jnp.bfloat16)
    weights = lax.dot_general(
        pick, packed[:, width : width + expert_total], NT, preferred_element_type=jnp.float32
    ) + lax.dot_general(
        pick, packed[:, width + expert_total :], NT, preferred_element_type=jnp.float32
    )
    x = packed[:, :width]
    for e in range(experts):
        if e >= head:
            up_copies[e - head].wait()
        rows = up_head[e] if e < head else up_tail[e - head]
        preact = lax.dot_general(rows, x, NT, preferred_element_type=jnp.float32)
        scaled = jnp.square(jnp.maximum(preact, 0.0)) * weights[e : e + 1, :]
        hidden[e] = scaled.astype(jnp.bfloat16)
    step = max(1, experts // 8)
    for e in range(0, experts, step):
        for copy in down_copies[e : e + step]:
            copy.wait()
        term = lax.dot_general(
            hidden[e : e + step].reshape(step * units, tokens),
            down_rows[e : e + step].reshape(step * units, width),
            TN,
            preferred_element_type=jnp.float32,
        )
        if e == 0:
            total[...] = term
        else:
            total[...] += term
    _, block_rows, quarter = partial.shape
    quarters = width // quarter
    for block in range(tokens // block_rows):
        place = block if flips is None else me ^ flips[block]
        for q in range(quarters):
            partial[place * quarters + q] = total[
                block * block_rows : (block + 1) * block_rows, q * quarter : (q + 1) * quarter
            ].astype(jnp.bfloat16)


def per_device(latents, expert_ids, gate_values, w_up, w_down):
    ep_count = lax.axis_size("ep")
    tp_count = lax.axis_size("tp")
    token_count, model_width = latents.shape
    experts, _, units = w_up.shape
    expert_total = experts * ep_count
    tokens = token_count * ep_count
    packed_width = model_width + 2 * expert_total
    up_rows = pltpu.with_memory_space_constraint(jnp.swapaxes(w_up, 1, 2), pltpu.HBM)
    down_rows = pltpu.with_memory_space_constraint(w_down, pltpu.HBM)
    head = max(1, experts * 5 // 8)
    row_bytes = 2 * units * model_width
    packed = pl.pallas_call(
        functools.partial(pack_kernel, expert_total),
        out_shape=jax.ShapeDtypeStruct((token_count, packed_width), jnp.bfloat16),
        in_specs=[HBM] * 3,
        out_specs=VMEM,
        scratch_shapes=[
            pltpu.VMEM(expert_ids.shape, jnp.int32),
            pltpu.VMEM(gate_values.shape, jnp.float32),
            pltpu.SemaphoreType.DMA((3,)),
        ],
        compiler_params=pltpu.CompilerParams(vmem_limit_bytes=2 << 20),
    )(*(pltpu.with_memory_space_constraint(a, pltpu.HBM) for a in (latents, expert_ids, gate_values)))

    def swap(rows, flip):
        return lax.ppermute(rows, "ep", [(i, i ^ flip) for i in range(ep_count)])

    direct = ep_count <= DIRECT
    chips = list(range(0, ep_count, 2))
    pieces = [packed]
    for s in chips[1:] if direct else ():
        pieces.append(swap(packed, s))
    up_head = pl.pallas_call(
        load_kernel,
        out_shape=pltpu.VMEM((head, units, model_width), jnp.bfloat16),
        in_specs=[HBM],
        out_specs=VMEM,
        scratch_shapes=[pltpu.SemaphoreType.DMA((head,))],
        compiler_params=pltpu.CompilerParams(vmem_limit_bytes=1 << 20),
        cost_estimate=pl.CostEstimate(flops=0, bytes_accessed=head * row_bytes, transcendentals=0),
    )(up_rows)
    if direct:
        own = jnp.concatenate(pieces)
        other = swap(own, 1)
        flips = chips + [s + 1 for s in chips]
    else:
        own, other = jnp.split(lax.all_gather(packed, "ep", axis=0, tiled=True), 2)
        flips = None
    partial = pl.pallas_call(
        functools.partial(expert_kernel, flips),
        out_shape=jax.ShapeDtypeStruct(
            (ep_count * tp_count, token_count, model_width // tp_count), jnp.bfloat16
        ),
        in_specs=[VMEM, VMEM, VMEM, HBM, HBM],
        out_specs=VMEM,
        scratch_shapes=[
            pltpu.VMEM((max(1, experts - head), units, model_width), jnp.bfloat16),
            pltpu.VMEM((experts, units, model_width), jnp.bfloat16),
            pltpu.VMEM((tokens, packed_width), jnp.bfloat16),
            pltpu.VMEM((experts, units, tokens), jnp.bfloat16),
            pltpu.VMEM((tokens, model_width), jnp.float32),
            pltpu.SemaphoreType.DMA((2, experts)),
        ],
        compiler_params=pltpu.CompilerParams(
            vmem_limit_bytes=(2 * experts - head) * row_bytes + (8 << 20)
            + 8 * tokens * packed_width
        ),
        cost_estimate=pl.CostEstimate(
            flops=4 * tokens * experts * units * model_width,
            bytes_accessed=(2 * experts - head) * row_bytes,
            transcendentals=0,
        ),
    )(own, other, up_head, up_rows, down_rows)
    received = lax.all_to_all(partial, ("ep", "tp"), split_axis=0, concat_axis=0, tiled=True)
    return jnp.sum(received.astype(jnp.float32), axis=0).astype(jnp.bfloat16)


def solution(mesh):
    return jax.shard_map(
        per_device,
        mesh=mesh,
        in_specs=(
            P("ep", None),
            P("ep", None),
            P("ep", None),
            P("ep", None, "tp"),
            P("ep", "tp", None),
        ),
        out_specs=P("ep", "tp"),
        check_vma=False,
    )
```

time: 87.5 us -> 43 us (0.49)
  waiting for transfers between devices: 28.7 us -> 3.65 us
  Pallas kernels: 0 us -> 20.5 us
  matrix products: 19.4 us -> 0 us
  between operations: 13.5 us -> 0.04 us
  blocking collectives: 17.5 us -> 13.2 us
  local copies, waits for them, and re-layouts: 3.63 us -> 0 us
  starting transfers between devices: 3.63 us -> 4.7 us
    reduce_scatter x1 -> x0, waiting for transfers between devices: 22.7 us -> none  [per_device(): lax.psum_scatter(partial_out.astype(jnp.bfloat16), 'tp', scatter_dimensio...]
    pallas_call x0 -> x3, Pallas kernels: none -> 20.5 us  [the longest x1 14.6 us: per_device(): pl.pallas_call(functools.partial(expert_kernel, flips), out_shape=jax.Sha...]
    dot_general x3 -> x0, matrix products: 19.4 us -> none  [the longest x1 18.2 us: expert_block(): jnp.einsum('abcf,bfk->abck', hidden, w_down, preferred_element_type=jnp.f...]
    all_to_all x1 -> x0, waiting for transfers between devices: 5.99 us -> none  [per_device(): lax.all_to_all(summed, 'ep', split_axis=0, concat_axis=0, tiled=True)]
    ppermute x0 -> x4, starting transfers between devices: none -> 4.7 us  [swap(): return lax.ppermute(rows, 'ep', [(i, i ^ flip) for i in range(ep_count)])]
    all_to_all x1, blocking collectives: 17.5 us -> 13.2 us  [per_device(): lax.all_to_all(partial, ('ep', 'tp'), split_axis=0, concat_axis=0, tiled=...]
    ppermute x0 -> x4, waiting for transfers between devices: none -> 3.65 us  [swap(): return lax.ppermute(rows, 'ep', [(i, i ^ flip) for i in range(ep_count)])]
    all_to_all x1 -> x0, starting transfers between devices: 3.63 us -> none  [per_device(): lax.all_to_all(summed, 'ep', split_axis=0, concat_axis=0, tiled=True)]
  transfers between devices with their start and end apart: 2 -> 4, of which waited for: 2 -> 3; matrix products, arithmetic and copies ran while one was open for 0% -> 0% of each run, Pallas kernels for 0% -> 12%
where the time goes in v1:
time: 43 us; the launch traced here: 42.8 us
  Pallas kernels  20.5 us (48%)
  blocking collectives  13.2 us (31%)
  starting transfers between devices  4.7 us (11%)
  waiting for transfers between devices  3.65 us (8%)
  other arithmetic  0.64 us (1%)
    pallas_call x1, Pallas kernels, per_device(): pl.pallas_call(functools.partial(expert_kernel, flips), out_shape=jax.Sha...  14.6 us
    all_to_all x1, blocking collectives, per_device(): lax.all_to_all(partial, ('ep', 'tp'), split_axis=0, concat_axis=0, tiled=...  13.2 us
    pallas_call x1, Pallas kernels, per_device(): pl.pallas_call(load_kernel, out_shape=pltpu.VMEM((head, units, model_widt...  5.04 us
    ppermute x4, starting transfers between devices, swap(): return lax.ppermute(rows, 'ep', [(i, i ^ flip) for i in range(ep_count)])  4.7 us
    ppermute x4, waiting for transfers between devices, swap(): return lax.ppermute(rows, 'ep', [(i, i ^ flip) for i in range(ep_count)])  3.65 us
    pallas_call x1, Pallas kernels, per_device(): pl.pallas_call(functools.partial(pack_kernel, expert_total), out_shape=ja...  0.87 us
  transfers between devices with their start and end apart: 4, of which 3 were waited for; matrix products, arithmetic and copies ran while one was open for 0% of the time, Pallas kernels for 12%

profile of v1, /device:TPU:0, one launch (start us, length us, event | category | flops | bytes accessed | tf_op | source)
XLA Modules:
  0.0 42.8 jit_solution(819730520203279728)
XLA Ops:
  0.0 0.9 %shard_map.55 = bf16[8,1280]{1,0:T(8,128)(2,1)S(1)} custom-call(bf16[8,1024]{1,0:T(8,128)(2,1)} %latents_hbm.1, s32[8,22]{1,0:T(8,128)} %ids_hbm.1, f32[8,22]{1,0:T(8,128)} %gates_hbm.1), custom_call_target="tpu_custom_call" | custom-call | tf_op jit(solution)/shard_map/pallas_call | solution.py:121
  0.9 4.0 %collective-permute-start.2 = (bf16[8,1280]{1,0:T(8,128)(2,1)S(1)}, bf16[8,1280]{1,0:T(8,128)(2,1)S(1)}, u32[]{:S(2)}, u32[]{:S(2)}) collective-permute-start(bf16[8,1280]{1,0:T(8,128)(2,1)S(1)} %shard_map.55), channel_id=1, source_target_pairs={{0,24},{4,28},{8,16},{12,20},{16,8},{20,12},{24,0},{28,4},{1,25},{... | collective-permute-start | bytes 61448 | tf_op jit(solution)/shard_map/ppermute | solution.py:135
  4.9 0.5 %collective-permute-start.1 = (bf16[8,1280]{1,0:T(8,128)(2,1)S(1)}, bf16[8,1280]{1,0:T(8,128)(2,1)S(1)}, u32[]{:S(2)}, u32[]{:S(2)}) collective-permute-start(bf16[8,1280]{1,0:T(8,128)(2,1)S(1)} %shard_map.55), channel_id=1, source_target_pairs={{0,16},{4,20},{8,24},{12,28},{16,0},{20,4},{24,8},{28,12},{1,17},{... | collective-permute-start | bytes 61448 | tf_op jit(solution)/shard_map/ppermute | solution.py:135
  5.4 0.1 collective-permute-start
  5.5 1.1 %collective-permute-done.2 = bf16[8,1280]{1,0:T(8,128)(2,1)S(1)} collective-permute-done((bf16[8,1280]{1,0:T(8,128)(2,1)S(1)}, bf16[8,1280]{1,0:T(8,128)(2,1)S(1)}, u32[]{:S(2)}, u32[]{:S(2)}) %collective-permute-start.2) | collective-permute-done | bytes 20512 | tf_op jit(solution)/shard_map/ppermute | solution.py:135
  6.6 2.0 %collective-permute-done.1 = bf16[8,1280]{1,0:T(8,128)(2,1)S(1)} collective-permute-done((bf16[8,1280]{1,0:T(8,128)(2,1)S(1)}, bf16[8,1280]{1,0:T(8,128)(2,1)S(1)}, u32[]{:S(2)}, u32[]{:S(2)}) %collective-permute-start.1) | collective-permute-done | bytes 20512 | tf_op jit(solution)/shard_map/ppermute | solution.py:135
  8.7 0.5 %collective-permute-done = bf16[8,1280]{1,0:T(8,128)(2,1)S(1)} collective-permute-done((bf16[8,1280]{1,0:T(8,128)(2,1)S(1)}, bf16[8,1280]{1,0:T(8,128)(2,1)S(1)}, u32[]{:S(2)}, u32[]{:S(2)}) %collective-permute-start) | collective-permute-done | bytes 20512 | tf_op jit(solution)/shard_map/ppermute | solution.py:135
  9.2 0.1 collective-permute-start.3
  9.2 5.0 %shard_map.56.up_head = bf16[10,672,1024]{2,1,0:T(8,128)(2,1)S(1)} custom-call(bf16[16,672,1024]{2,1,0:T(8,128)(2,1)} %bitcast.1), custom_call_target="tpu_custom_call" | custom-call | bytes 13762560 | tf_op jit(solution)/shard_map/pallas_call | solution.py:142
  14.3 0.0 collective-permute-done.3.other
  14.3 14.6 %shard_map.57 = bf16[32,8,256]{2,1,0:T(8,128)(2,1)S(1)} custom-call(bf16[32,1280]{1,0:T(8,128)(2,1)S(1)} %pad_maximum_fusion.own, bf16[32,1280]{1,0:T(8,128)(2,1)S(1)} %collective-permute-done.3.other, bf16[10,672,1024]{2,1,0:T(8,128)(2,1)S(1)} %shard_map.56.up_head, bf16[16,672,1024]{2,1,0:T(8,128)(2,1)} %bitcast.2, bf16[16,672,1024]{2,1,0:T(8,128)(2,1)} %down_hbm.1), custom_call_target="tpu_custom_call" | custom-call | flops 2818572288 | bytes 30277632 | tf_op jit(solution)/shard_map/pallas_call | solution.py:158
  28.9 13.2 %all_to_all.5 = bf16[32,8,256]{2,1,0:T(8,128)(2,1)S(1)} all-to-all(bf16[32,8,256]{2,1,0:T(8,128)(2,1)S(1)} %shard_map.57), channel_id=1, replica_groups=mesh['ep'=8,'tp'=4] {'ep','tp'}, dimensions={0} | all-to-all | bytes 262144 | tf_op jit(solution)/shard_map/all_to_all | solution.py:183
  42.1 0.6 %reduce_sum.12 = bf16[8,256]{1,0:T(8,128)(2,1)} reduce(bf16[32,8,256]{2,1,0:T(8,128)(2,1)S(1)} %all_to_all.5, bf16[]{:T(256)} %constant.2.clone.1), dimensions={0}, to_apply=%region_0.0 | reduce | flops 63488 | bytes 135170 | tf_op jit(solution)/shard_map/reduce_sum | solution.py:184
  (1 shorter events, 0.0 us)
Async XLA Ops:
  0.9 5.8 %collective-permute-start.2 = (bf16[8,1280]{1,0:T(8,128)(2,1)S(1)}, bf16[8,1280]{1,0:T(8,128)(2,1)S(1)}, u32[]{:S(2)}, u32[]{:S(2)}) collective-permute-start(bf16[8,1280]{1,0:T(8,128)(2,1)S(1)} %shard_map.55), channel_id=1, source_target_pairs={{0,24},{4,28},{8,16},{12,20},{16,8},{20,12},{24,0},{28,4},{1,25},{... | collective-permute-start | bytes 61448 | tf_op jit(solution)/shard_map/ppermute | solution.py:135
  4.9 3.8 %collective-permute-start.1 = (bf16[8,1280]{1,0:T(8,128)(2,1)S(1)}, bf16[8,1280]{1,0:T(8,128)(2,1)S(1)}, u32[]{:S(2)}, u32[]{:S(2)}) collective-permute-start(bf16[8,1280]{1,0:T(8,128)(2,1)S(1)} %shard_map.55), channel_id=1, source_target_pairs={{0,16},{4,20},{8,24},{12,28},{16,0},{20,4},{24,8},{28,12},{1,17},{... | collective-permute-start | bytes 61448 | tf_op jit(solution)/shard_map/ppermute | solution.py:135
  5.4 3.8 %collective-permute-start = (bf16[8,1280]{1,0:T(8,128)(2,1)S(1)}, bf16[8,1280]{1,0:T(8,128)(2,1)S(1)}, u32[]{:S(2)}, u32[]{:S(2)}) collective-permute-start(bf16[8,1280]{1,0:T(8,128)(2,1)S(1)} %shard_map.55), channel_id=1, source_target_pairs={{0,8},{4,12},{8,0},{12,4},{16,24},{20,28},{24,16},{28,20},{1,9},{5... | collective-permute-start | bytes 61448 | tf_op jit(solution)/shard_map/ppermute | solution.py:135
  9.2 5.1 %collective-permute-start.3 = (bf16[32,1280]{1,0:T(8,128)(2,1)S(1)}, bf16[32,1280]{1,0:T(8,128)(2,1)S(1)}, u32[]{:S(2)}, u32[]{:S(2)}) collective-permute-start(bf16[32,1280]{1,0:T(8,128)(2,1)S(1)} %pad_maximum_fusion.own), channel_id=1, source_target_pairs={{0,4},{4,0},{8,12},{12,8},{16,20},{20,16},{24,28},{28,24},{1,5},{5... | collective-permute-start | bytes 245768 | tf_op jit(solution)/shard_map/ppermute | solution.py:135

commit v2 on v1

--- a/solution.py
+++ b/solution.py
@@ -46,23 +46,31 @@
         copy.wait()
 
 
-def expert_kernel(flips, own, other, up_head, up_hbm, down_hbm, partial, up_tail, down_rows, packed, hidden, total, sems):
+def expert_kernel(flips, *refs):
+    *pieces, up_head, up_hbm, down_hbm, partial = refs[:-6]
+    up_tail, down_rows, packed, hidden, total, sems = refs[-6:]
     experts, units, width = down_hbm.shape
     head = up_head.shape[0]
     tokens = packed.shape[0]
     expert_total = (packed.shape[1] - width) // 2
-    up_copies = [
-        pltpu.make_async_copy(up_hbm.at[e], up_tail.at[e - head], sems.at[0, e])
-        for e in range(head, experts)
-    ]
-    down_copies = [
-        pltpu.make_async_copy(down_hbm.at[e], down_rows.at[e], sems.at[1, e])
-        for e in range(experts)
-    ]
-    for copy in up_copies + down_copies:
-        copy.start()
-    packed[: own.shape[0]] = own[...]
-    packed[own.shape[0] :] = other[...]
+
+    def up_copy(e):
+        return pltpu.make_async_copy(up_hbm.at[e], up_tail.at[e - head], sems.at[0, e])
+
+    def down_copy(e):
+        return pltpu.make_async_copy(down_hbm.at[e], down_rows.at[e], sems.at[1, e])
+
+    @pl.loop(head, experts)
+    def _(e):
+        up_copy(e).start()
+
+    @pl.loop(0, experts)
+    def _(e):
+        down_copy(e).start()
+
+    each = pieces[0].shape[0]
+    for i, piece in enumerate(pieces):
+        packed[i * each : (i + 1) * each] = piece[...]
     me = lax.axis_index("ep")
     shape = (max(8, experts), expert_total)
     pick = lax.broadcasted_iota(jnp.int32, shape, 1) == (
@@ -76,16 +84,17 @@
     )
     x = packed[:, :width]
     for e in range(experts):
-        if e >= head:
-            up_copies[e - head].wait()
+        if e == head:
+            for i in range(head, experts):
+                up_copy(i).wait()
         rows = up_head[e] if e < head else up_tail[e - head]
         preact = lax.dot_general(rows, x, NT, preferred_element_type=jnp.float32)
         scaled = jnp.square(jnp.maximum(preact, 0.0)) * weights[e : e + 1, :]
         hidden[e] = scaled.astype(jnp.bfloat16)
     step = max(1, experts // 8)
     for e in range(0, experts, step):
-        for copy in down_copies[e : e + step]:
-            copy.wait()
+        for i in range(e, e + step):
+            down_copy(i).wait()
         term = lax.dot_general(
             hidden[e : e + step].reshape(step * units, tokens),
             down_rows[e : e + step].reshape(step * units, width),
@@ -136,9 +145,14 @@
 
     direct = ep_count <= DIRECT
     chips = list(range(0, ep_count, 2))
-    pieces = [packed]
-    for s in chips[1:] if direct else ():
-        pieces.append(swap(packed, s))
+    if direct:
+        pieces = [jnp.concatenate([packed, swap(packed, 1)])]
+        for s in chips[1:]:
+            pieces.append(swap(pieces[0], s))
+        flips = [s + core for s in chips for core in range(2)]
+    else:
+        pieces = [lax.all_gather(packed, "ep", axis=0, tiled=True)]
+        flips = None
     up_head = pl.pallas_call(
         load_kernel,
         out_shape=pltpu.VMEM((head, units, model_width), jnp.bfloat16),
@@ -148,19 +162,12 @@
         compiler_params=pltpu.CompilerParams(vmem_limit_bytes=1 << 20),
         cost_estimate=pl.CostEstimate(flops=0, bytes_accessed=head * row_bytes, transcendentals=0),
     )(up_rows)
-    if direct:
-        own = jnp.concatenate(pieces)
-        other = swap(own, 1)
-        flips = chips + [s + 1 for s in chips]
-    else:
-        own, other = jnp.split(lax.all_gather(packed, "ep", axis=0, tiled=True), 2)
-        flips = None
     partial = pl.pallas_call(
         functools.partial(expert_kernel, flips),
         out_shape=jax.ShapeDtypeStruct(
             (ep_count * tp_count, token_count, model_width // tp_count), jnp.bfloat16
         ),
-        in_specs=[VMEM, VMEM, VMEM, HBM, HBM],
+        in_specs=[VMEM] * (len(pieces) + 1) + [HBM] * 2,
         out_specs=VMEM,
         scratch_shapes=[
             pltpu.VMEM((max(1, experts - head), units, model_width), jnp.bfloat16),
@@ -179,7 +186,7 @@
             bytes_accessed=(2 * experts - head) * row_bytes,
             transcendentals=0,
         ),
-    )(own, other, up_head, up_rows, down_rows)
+    )(*pieces, up_head, up_rows, down_rows)
     received = lax.all_to_all(partial, ("ep", "tp"), split_axis=0, concat_axis=0, tiled=True)
     return jnp.sum(received.astype(jnp.float32), axis=0).astype(jnp.bfloat16)
 

time: 43 us -> 37.9 us (0.88)
  Pallas kernels: 20.5 us -> 16.7 us
  waiting for transfers between devices: 3.65 us -> 0.85 us
  blocking collectives: 13.2 us -> 14.4 us
    pallas_call x1, Pallas kernels: 14.6 us -> 10.8 us  [per_device(): pl.pallas_call(functools.partial(expert_kernel, flips), out_shape=jax.Sha...]
    ppermute x4, waiting for transfers between devices: 3.65 us -> 0.85 us  [swap(): return lax.ppermute(rows, 'ep', [(i, i ^ flip) for i in range(ep_count)])]
    all_to_all x1, blocking collectives: 13.2 us -> 14.4 us  [per_device(): lax.all_to_all(partial, ('ep', 'tp'), split_axis=0, concat_axis=0, tiled=...]
  transfers between devices with their start and end apart: 4 -> 4, of which waited for: 3 -> 1; matrix products, arithmetic and copies ran while one was open for 0% -> 0% of each run, Pallas kernels for 12% -> 13%
where the time goes in v2:
time: 37.9 us; the launch traced here: 37.7 us
  Pallas kernels  16.7 us (44%)
  blocking collectives  14.4 us (38%)
  starting transfers between devices  4.96 us (13%)
  waiting for transfers between devices  0.85 us (2%)
  other arithmetic  0.63 us (2%)
    all_to_all x1, blocking collectives, per_device(): lax.all_to_all(partial, ('ep', 'tp'), split_axis=0, concat_axis=0, tiled=...  14.4 us
    pallas_call x1, Pallas kernels, per_device(): pl.pallas_call(functools.partial(expert_kernel, flips), out_shape=jax.Sha...  10.8 us
    pallas_call x1, Pallas kernels, per_device(): pl.pallas_call(load_kernel, out_shape=pltpu.VMEM((head, units, model_widt...  5.04 us
    ppermute x4, starting transfers between devices, swap(): return lax.ppermute(rows, 'ep', [(i, i ^ flip) for i in range(ep_count)])  4.96 us
    pallas_call x1, Pallas kernels, per_device(): pl.pallas_call(functools.partial(pack_kernel, expert_total), out_shape=ja...  0.87 us
    ppermute x4, waiting for transfers between devices, swap(): return lax.ppermute(rows, 'ep', [(i, i ^ flip) for i in range(ep_count)])  0.85 us
  transfers between devices with their start and end apart: 4, of which 1 were waited for; matrix products, arithmetic and copies ran while one was open for 0% of the time, Pallas kernels for 13%

profile of v2, /device:TPU:0, one launch (start us, length us, event | category | flops | bytes accessed | tf_op | source)
XLA Modules:
  0.0 37.7 jit_solution(14465681882593108131)
XLA Ops:
  0.0 0.9 %shard_map.55 = bf16[8,1280]{1,0:T(8,128)(2,1)S(1)} custom-call(bf16[8,1024]{1,0:T(8,128)(2,1)} %latents_hbm.1, s32[8,22]{1,0:T(8,128)} %ids_hbm.1, f32[8,22]{1,0:T(8,128)} %gates_hbm.1), custom_call_target="tpu_custom_call" | custom-call | tf_op jit(solution)/shard_map/pallas_call | solution.py:130
  0.9 0.6 %collective-permute-start = (bf16[8,1280]{1,0:T(8,128)(2,1)S(1)}, bf16[8,1280]{1,0:T(8,128)(2,1)S(1)}, u32[]{:S(2)}, u32[]{:S(2)}) collective-permute-start(bf16[8,1280]{1,0:T(8,128)(2,1)S(1)} %shard_map.55), channel_id=1, source_target_pairs={{0,4},{4,0},{8,12},{12,8},{16,20},{20,16},{24,28},{28,24},{1,5},{5... | collective-permute-start | bytes 61448 | tf_op jit(solution)/shard_map/ppermute | solution.py:144
  1.4 0.8 %collective-permute-done = bf16[8,1280]{1,0:T(8,128)(2,1)S(1)} collective-permute-done((bf16[8,1280]{1,0:T(8,128)(2,1)S(1)}, bf16[8,1280]{1,0:T(8,128)(2,1)S(1)}, u32[]{:S(2)}, u32[]{:S(2)}) %collective-permute-start) | collective-permute-done | bytes 20512 | tf_op jit(solution)/shard_map/ppermute | solution.py:144
  2.3 3.8 %collective-permute-start.3 = (bf16[16,1280]{1,0:T(8,128)(2,1)S(1)}, bf16[16,1280]{1,0:T(8,128)(2,1)S(1)}, u32[]{:S(2)}, u32[]{:S(2)}) collective-permute-start(bf16[16,1280]{1,0:T(8,128)(2,1)S(1)} %pad_maximum_fusion.refs_0_), channel_id=1, source_target_pairs={{0,24},{4,28},{8,16},{12,20},{16,8},{20,12},{24,0},{28,4},{1,25},{... | collective-permute-start | bytes 122888 | tf_op jit(solution)/shard_map/ppermute | solution.py:144
  6.1 0.5 %collective-permute-start.2 = (bf16[16,1280]{1,0:T(8,128)(2,1)S(1)}, bf16[16,1280]{1,0:T(8,128)(2,1)S(1)}, u32[]{:S(2)}, u32[]{:S(2)}) collective-permute-start(bf16[16,1280]{1,0:T(8,128)(2,1)S(1)} %pad_maximum_fusion.refs_0_), channel_id=1, source_target_pairs={{0,16},{4,20},{8,24},{12,28},{16,0},{20,4},{24,8},{28,12},{1,17},{... | collective-permute-start | bytes 122888 | tf_op jit(solution)/shard_map/ppermute | solution.py:144
  6.6 0.1 collective-permute-start.1
  6.7 5.0 %shard_map.56.refs_4_ = bf16[10,672,1024]{2,1,0:T(8,128)(2,1)S(1)} custom-call(bf16[16,672,1024]{2,1,0:T(8,128)(2,1)} %bitcast.1), custom_call_target="tpu_custom_call" | custom-call | bytes 13762560 | tf_op jit(solution)/shard_map/pallas_call | solution.py:156
  11.7 0.0 collective-permute-done.3.refs_3_
  11.7 0.0 collective-permute-done.2.refs_2_
  11.8 0.0 collective-permute-done.1.refs_1_
  11.8 10.8 %shard_map.57 = bf16[32,8,256]{2,1,0:T(8,128)(2,1)S(1)} custom-call(bf16[16,1280]{1,0:T(8,128)(2,1)S(1)} %pad_maximum_fusion.refs_0_, bf16[16,1280]{1,0:T(8,128)(2,1)S(1)} %collective-permute-done.1.refs_1_, bf16[16,1280]{1,0:T(8,128)(2,1)S(1)} %collective-permute-done.2.refs_2_, bf16[16,1280]{1,0:T(8,128)(2,1)S(1)} %collective-permute-done.3.refs_3_, ...), custom_call_target="tpu_custom_call" | custom-call | flops 2818572288 | bytes 30277632 | tf_op jit(solution)/shard_map/pallas_call | solution.py:165
  22.6 14.4 %all_to_all.5 = bf16[32,8,256]{2,1,0:T(8,128)(2,1)S(1)} all-to-all(bf16[32,8,256]{2,1,0:T(8,128)(2,1)S(1)} %shard_map.57), channel_id=1, replica_groups=mesh['ep'=8,'tp'=4] {'ep','tp'}, dimensions={0} | all-to-all | bytes 262144 | tf_op jit(solution)/shard_map/all_to_all | solution.py:190
  37.0 0.6 %reduce_sum.12 = bf16[8,256]{1,0:T(8,128)(2,1)} reduce(bf16[32,8,256]{2,1,0:T(8,128)(2,1)S(1)} %all_to_all.5, bf16[]{:T(256)} %constant.2.clone.1), dimensions={0}, to_apply=%region_0.0 | reduce | flops 63488 | bytes 135170 | tf_op jit(solution)/shard_map/reduce_sum | solution.py:191
  (1 shorter events, 0.0 us)
Async XLA Ops:
  0.9 1.4 %collective-permute-start = (bf16[8,1280]{1,0:T(8,128)(2,1)S(1)}, bf16[8,1280]{1,0:T(8,128)(2,1)S(1)}, u32[]{:S(2)}, u32[]{:S(2)}) collective-permute-start(bf16[8,1280]{1,0:T(8,128)(2,1)S(1)} %shard_map.55), channel_id=1, source_target_pairs={{0,4},{4,0},{8,12},{12,8},{16,20},{20,16},{24,28},{28,24},{1,5},{5... | collective-permute-start | bytes 61448 | tf_op jit(solution)/shard_map/ppermute | solution.py:144
  2.3 9.4 %collective-permute-start.3 = (bf16[16,1280]{1,0:T(8,128)(2,1)S(1)}, bf16[16,1280]{1,0:T(8,128)(2,1)S(1)}, u32[]{:S(2)}, u32[]{:S(2)}) collective-permute-start(bf16[16,1280]{1,0:T(8,128)(2,1)S(1)} %pad_maximum_fusion.refs_0_), channel_id=1, source_target_pairs={{0,24},{4,28},{8,16},{12,20},{16,8},{20,12},{24,0},{28,4},{1,25},{... | collective-permute-start | bytes 122888 | tf_op jit(solution)/shard_map/ppermute | solution.py:144
  6.1 5.7 %collective-permute-start.2 = (bf16[16,1280]{1,0:T(8,128)(2,1)S(1)}, bf16[16,1280]{1,0:T(8,128)(2,1)S(1)}, u32[]{:S(2)}, u32[]{:S(2)}) collective-permute-start(bf16[16,1280]{1,0:T(8,128)(2,1)S(1)} %pad_maximum_fusion.refs_0_), channel_id=1, source_target_pairs={{0,16},{4,20},{8,24},{12,28},{16,0},{20,4},{24,8},{28,12},{1,17},{... | collective-permute-start | bytes 122888 | tf_op jit(solution)/shard_map/ppermute | solution.py:144
  6.6 5.2 %collective-permute-start.1 = (bf16[16,1280]{1,0:T(8,128)(2,1)S(1)}, bf16[16,1280]{1,0:T(8,128)(2,1)S(1)}, u32[]{:S(2)}, u32[]{:S(2)}) collective-permute-start(bf16[16,1280]{1,0:T(8,128)(2,1)S(1)} %pad_maximum_fusion.refs_0_), channel_id=1, source_target_pairs={{0,8},{4,12},{8,0},{12,4},{16,24},{20,28},{24,16},{28,20},{1,9},{5... | collective-permute-start | bytes 122888 | tf_op jit(solution)/shard_map/ppermute | solution.py:144
